TPU v7x, 512 devices: a whole 4x8x8 slice. The times are simulated.
512 devices in a mesh: row: 32 (over y, x_hi, core), col: 16 (over z, x_lo).
Axes of the slice: x: 4 (x_hi: 2, x_lo: 2; x = x_hi * 2 + x_lo), y: 8, z: 8, core: 2. Of those that a mesh axis runs over, the one named last changes fastest.
Arguments:
- features: bfloat16 [65536, 512], P(('col', 'row')), may hold values from -6 to 6
- block_values: bfloat16 [32, 16, 12, 128, 128], P('row', 'col'), may hold values from -0.21875 to 0.21875
- block_rows: int32 [32, 16, 12], P('row', 'col'), may hold values from 0 to 15
- block_cols: int32 [32, 16, 12], P('row', 'col'), may hold values from 0 to 31
- block_count: int32 [32, 16], P('row', 'col'), may hold values from 3 to 12, as said below
- weight: bfloat16 [512, 512], replicated, may hold values from -0.25 to 0.25
- bias: float32 [512], replicated, may hold values from -3 to 3
- cotangent: bfloat16 [65536, 512], P(('row', 'col')), may hold values from -6 to 6
Outputs:
- hidden: bfloat16 [65536, 512], P(('row', 'col'))
- weight_grad: float32 [512, 512], replicated
- bias_grad: float32 [512], replicated
- feature_grad: bfloat16 [65536, 512], P(('col', 'row'))
Inputs may be any that keep to these rules, and one draw needn't show every extreme that they name: `block_count`: no grid tile has more than 12 live slots, and some tile has exactly 12.
All inputs are finite; a program needn't handle non-finite values.
Results may differ from a plain program's by a relative error of at most 0.017.
Values may be sent and summed in bfloat16 or wider, within the bound.
A program may use at most 64 MiB of HBM per device.

v0:
```python
import jax
import jax.numpy as jnp
from jax import lax
from jax.sharding import PartitionSpec as P


def slot_product(tile_values, tile_rows, tile_cols, live_count, source, out_len, backward):
    capacity = tile_values.shape[0]
    block_size = tile_values.shape[1]
    width = source.shape[1]
    group = max([d for d in range(1, min(capacity, 16) + 1) if capacity % d == 0])
    groups = capacity // group
    panels = source.reshape(source.shape[0] // block_size, block_size, width)
    out_blocks = out_len // block_size
    if backward:
        source_ids = tile_rows
        target_ids = tile_cols
        form = "sba,sbf->saf"
    else:
        source_ids = tile_cols
        target_ids = tile_rows
        form = "sab,sbf->saf"
    alive = jnp.arange(capacity, dtype=jnp.int32) < live_count
    places = jnp.arange(out_blocks, dtype=jnp.int32)

    def one_group(total, items):
        values_part, source_part, target_part, alive_part = items
        segments = jnp.take(panels, source_part, axis=0)
        products = jnp.einsum(form, values_part, segments, preferred_element_type=jnp.float32)
        selector = ((target_part[None, :] == places[:, None]) & alive_part[None, :]).astype(
            jnp.float32
        )
        added = jnp.einsum("rs,saf->raf", selector, products, precision=lax.Precision.HIGHEST)
        return (total + added, None)

    items = (
        tile_values.reshape(groups, group, block_size, block_size),
        source_ids.reshape(groups, group),
        target_ids.reshape(groups, group),
        alive.reshape(groups, group),
    )
    start = jnp.zeros((out_blocks, block_size, width), jnp.float32)
    total, _ = lax.scan(one_group, start, items)
    return total.reshape(out_len, width)


def global_grads(local_weight, local_bias):
    return lax.psum((local_weight, local_bias), ("row", "col"))


def transposed_product(left, weight):
    return lax.dot_general(
        left, weight, (((1,), (1,)), ((), ())), preferred_element_type=jnp.float32
    ).astype(jnp.bfloat16)


def source_total(received):
    return jnp.sum(received.astype(jnp.float32), axis=0).astype(jnp.bfloat16)


def per_device(
    features, block_values, block_rows, block_cols, block_count, weight, bias, cotangent
):
    tile_values = block_values[0, 0]
    tile_rows = block_rows[0, 0]
    tile_cols = block_cols[0, 0]
    live_count = block_count[0, 0]
    own_nodes = features.shape[0]
    width = features.shape[1]
    row_len = lax.axis_size("col") * own_nodes
    gathered = lax.all_gather(features, "row", axis=0, tiled=True)
    col_len = gathered.shape[0]
    partial_value = slot_product(
        tile_values, tile_rows, tile_cols, live_count, gathered, row_len, False
    )
    aggregate = lax.psum_scatter(
        partial_value.astype(jnp.bfloat16), "col", scatter_dimension=0, tiled=True
    )
    preact = jnp.dot(aggregate, weight, preferred_element_type=jnp.float32) + bias
    hidden = jax.nn.silu(preact).astype(jnp.bfloat16)
    sigma = jax.nn.sigmoid(preact)
    grad_pre = cotangent.astype(jnp.float32) * sigma * (1.0 + preact * (1.0 - sigma))
    grad_low = grad_pre.astype(jnp.bfloat16)
    local_weight = lax.dot_general(
        aggregate, grad_low, (((0,), (0,)), ((), ())), preferred_element_type=jnp.float32
    )
    local_bias = jnp.sum(grad_pre, axis=0)
    grad_agg = transposed_product(grad_low, weight)
    grad_panel = lax.all_gather(grad_agg, "col", axis=0, tiled=True)
    back = slot_product(tile_values, tile_rows, tile_cols, live_count, grad_panel, col_len, True)
    back_low = back.astype(jnp.bfloat16).reshape(col_len // own_nodes, own_nodes, width)
    received = lax.all_to_all(back_low, "row", split_axis=0, concat_axis=0, tiled=True)
    feature_grad = source_total(received)
    weight_grad, bias_grad = global_grads(local_weight, local_bias)
    return (hidden, weight_grad, bias_grad, feature_grad)


def solution(mesh):
    in_specs = (
        P(("col", "row"), None),
        P("row", "col", None, None, None),
        P("row", "col", None),
        P("row", "col", None),
        P("row", "col"),
        P(),
        P(),
        P(("row", "col"), None),
    )
    out_specs = (P(("row", "col"), None), P(), P(), P(("col", "row"), None))
    return jax.shard_map(
        per_device, mesh=mesh, in_specs=in_specs, out_specs=out_specs, check_vma=False
    )
```

profile of v0, /device:TPU:24, one launch (start us, length us, event | category | flops | bytes accessed | tf_op | source)
XLA Modules:
  0.0 616.6 jit_solution(6726816917784381716)
XLA Ops:
  7.2 0.7 all-gather.3.cloned.1.call-update
  8.6 0.7 fusion.21
  9.3 0.7 compare_and_fusion.1
  10.0 97.7 %all-gather.3.cloned.1.call-done = bf16[4096,512]{1,0:T(8,128)(2,1)} async-done(((bf16[128,512]{1,0:T(8,128)(2,1)}), bf16[4096,512]{1,0:T(8,128)(2,1)}) %all-gather.3.cloned.1.call-update) | async-done | bytes 4194320 | tf_op jit(solution)/shard_map/all_gather | solution.py:71
  107.6 2.8 gather_fusion
  110.5 2.4 convolution_bitcast_fusion.1
  112.9 5.2 copy.18
  118.1 4.3 convolution_convert_fusion.1
  122.5 2.5 copy.19
  125.1 76.2 %reduce-scatter.2.cloned.1.call-done = bf16[128,512]{1,0:T(8,128)(2,1)} async-done(((bf16[2048,512]{1,0:T(8,128)(2,1)}), bf16[128,512]{1,0:T(8,128)(2,1)}) %reduce-scatter.2.cloned.1.call-update) | async-done | bytes 131088 | tf_op jit(solution)/shard_map/reduce_scatter | solution.py:76
  201.3 1.9 fusion.25
  203.2 1.0 convolution_convert_fusion.2
  204.2 74.5 %all-gather.5.cloned.1.call-done = bf16[2048,512]{1,0:T(8,128)(2,1)} async-done(((bf16[128,512]{1,0:T(8,128)(2,1)}), bf16[2048,512]{1,0:T(8,128)(2,1)}) %all-gather.5.cloned.1.call-update) | async-done | bytes 2097168 | tf_op jit(solution)/shard_map/all_gather | solution.py:89
  278.8 2.2 gather_fusion.1
  281.0 2.4 convolution_bitcast_fusion
  283.4 5.2 copy.21
  288.6 5.5 convolution_convert_fusion
  294.2 4.4 copy.22
  298.5 9.7 %all-to-all-start = ((bf16[32,128,512]{2,1,0:T(8,128)(2,1)}), bf16[32,128,512]{2,1,0:T(8,128)(2,1)}, u32[]{:S(2)}, u32[]{:S(2)}) async-start(bf16[32,128,512]{2,1,0:T(8,128)(2,1)} %copy.22), calls=%async_computation.1 | async-start | bytes 8388608 | tf_op jit(solution)/shard_map/all_to_all | solution.py:92
  308.3 1.3 fusion.9
  309.6 183.3 %psum.15 = f32[512]{0:T(512)} all-reduce(f32[512]{0:T(512)S(1)} %get-tuple-element.36), channel_id=1, replica_groups=mesh['row'=32,'col'=16] {'row','col'}, use_global_device_ids=true, to_apply=%region_3.4 | all-reduce | flops 512 | bytes 4096 | tf_op jit(solution)/shard_map/psum | solution.py:48
  492.9 3.5 reduce_sum.22
  496.4 111.4 %all-reduce.2.cloned.1.call-done = f32[512,512]{1,0:T(8,128)} async-done(((f32[512,512]{1,0:T(8,128)}), f32[512,512]{1,0:T(8,128)}) %all-reduce.2.cloned.1.call-update) | async-done | bytes 1048592 | tf_op jit(solution)/shard_map/psum | solution.py:48
  607.8 2.3 copy.27
  (27 shorter events, 0.3 us)
Async XLA Ops:
  7.2 194.1 %copy-start = (bf16[512,512]{1,0:T(8,128)(2,1)S(1)}, bf16[512,512]{1,0:T(8,128)(2,1)}, u32[]{:S(2)}) copy-start(bf16[512,512]{1,0:T(8,128)(2,1)} %param.13) | copy-start | bytes 1572868
  7.2 103.3 %copy-start.1 = (bf16[1,1,12,128,128]{4,3,2,1,0:T(8,128)(2,1)S(1)}, bf16[1,1,12,128,128]{4,3,2,1,0:T(8,128)(2,1)}, u32[]{:S(2)}) copy-start(bf16[1,1,12,128,128]{4,3,2,1,0:T(8,128)(2,1)} %param.9) | copy-start | bytes 1179652
  7.2 100.5 %all-gather.3.cloned.1.call-start = ((), (), s32[]{:S(2)}) async-start(), calls=%async_computation.2 | async-start | bytes 4325376 | tf_op jit(solution)/shard_map/all_gather | solution.py:71
  7.9 193.4 %reduce-scatter.2.cloned.1.call-start = ((), (), s32[]{:S(2)}) async-start(), calls=%async_computation.3 | async-start | bytes 2228224 | tf_op jit(solution)/shard_map/reduce_scatter | solution.py:76
  112.9 5.3 copy-start.4
  125.0 76.3 %copy-start.5 = (bf16[128,512]{1,0:T(8,128)(2,1)S(1)}, bf16[128,512]{1,0:T(8,128)(2,1)}, u32[]{:S(2)}) copy-start(bf16[128,512]{1,0:T(8,128)(2,1)} %param.15) | copy-start | bytes 393220
  125.0 76.3 %copy-start.6 = (f32[512]{0:T(512)S(1)}, f32[512]{0:T(512)}, u32[]{:S(2)}) copy-start(f32[512]{0:T(512)} %param.14) | copy-start | bytes 6148
  125.0 153.8 %all-gather.5.cloned.1.call-start = ((), (), s32[]{:S(2)}) async-start(), calls=%async_computation.5 | async-start | bytes 2228224 | tf_op jit(solution)/shard_map/all_gather | solution.py:89
  283.4 5.3 copy-start.3
  298.5 9.7 %copy-start.2 = (bf16[128,512]{1,0:T(8,128)(2,1)S(1)}, bf16[128,512]{1,0:T(8,128)(2,1)}, u32[]{:S(2)}) copy-start(bf16[128,512]{1,0:T(8,128)(2,1)} %reduce-scatter.2.cloned.1.call-done) | copy-start | bytes 393220
  298.5 194.4 %all-to-all-start = ((bf16[32,128,512]{2,1,0:T(8,128)(2,1)}), bf16[32,128,512]{2,1,0:T(8,128)(2,1)}, u32[]{:S(2)}, u32[]{:S(2)}) async-start(bf16[32,128,512]{2,1,0:T(8,128)(2,1)} %copy.22), calls=%async_computation.1 | async-start | bytes 8388608 | tf_op jit(solution)/shard_map/all_to_all | solution.py:92
  308.2 299.5 %all-reduce.2.cloned.1.call-start = ((), (), s32[]{:S(2)}) async-start(), calls=%async_computation.4 | async-start | bytes 2097152 | tf_op jit(solution)/shard_map/psum | solution.py:48
Sparse Core Ops, SparseCore 0:
  11.4 96.2 all-gather.2
  125.1 76.1 reduce-scatter.1
  204.3 74.4 all-gather.4
  314.4 293.3 all-reduce.1
where the time goes:
time: 617 us
  waiting for transfers between devices  361 us (59%)
  blocking collectives  183 us (30%)
  local copies, waits for them, and re-layouts  24.8 us (4%)
  matrix products  18.8 us (3%)
  between operations  14.5 us (2%)
  starting transfers between devices  9.84 us (2%)
    psum x1, blocking collectives, global_grads(): return lax.psum((local_weight, local_bias), ('row', 'col'))  183 us
    psum x1, waiting for transfers between devices, global_grads(): return lax.psum((local_weight, local_bias), ('row', 'col'))  111 us
    all_gather x1, waiting for transfers between devices, per_device(): gathered = lax.all_gather(features, 'row', axis=0, tiled=True)  97.7 us
    reduce_scatter x1, waiting for transfers between devices, per_device(): lax.psum_scatter(partial_value.astype(jnp.bfloat16), 'col', scatter_dimen...  76.2 us
    all_gather x1, waiting for transfers between devices, per_device(): grad_panel = lax.all_gather(grad_agg, 'col', axis=0, tiled=True)  74.5 us
  transfers between devices with their start and end apart: 5, of which 4 were waited for; matrix products, arithmetic and copies ran while one was open for 1% of the time, Pallas kernels for 0%

commit v1 on v0

--- a/solution.py
+++ b/solution.py
@@ -2,6 +2,11 @@
 import jax.numpy as jnp
 from jax import lax
 from jax.sharding import PartitionSpec as P
+
+
+def axis_by_axis(x, inner_axis, outer_axis):
+    partial = lax.psum(x, inner_axis)
+    return lax.psum(partial, outer_axis)
 
 
 def slot_product(tile_values, tile_rows, tile_cols, live_count, source, out_len, backward):
@@ -45,7 +50,7 @@
 
 
 def global_grads(local_weight, local_bias):
-    return lax.psum((local_weight, local_bias), ("row", "col"))
+    return axis_by_axis((local_weight, local_bias), "row", "col")
 
 
 def transposed_product(left, weight):

time: 617 us -> 764 us (1.24)
  the two profiles are of different devices: /device:TPU:24 before, /device:TPU:8 now
where the time goes in v1:
time: 764 us
  waiting for transfers between devices  587 us (77%)
  blocking collectives  104 us (14%)
  local copies, waits for them, and re-layouts  24.7 us (3%)
  matrix products  18.8 us (2%)
  between operations  14.5 us (2%)
  starting transfers between devices  10.1 us (1%)
    psum x1, waiting for transfers between devices, axis_by_axis(): partial = lax.psum(x, inner_axis)  291 us
    all_gather x1, waiting for transfers between devices, per_device(): gathered = lax.all_gather(features, 'row', axis=0, tiled=True)  97.8 us
    reduce_scatter x1, waiting for transfers between devices, per_device(): lax.psum_scatter(partial_value.astype(jnp.bfloat16), 'col', scatter_dimen...  76.2 us
    all_gather x1, waiting for transfers between devices, per_device(): grad_panel = lax.all_gather(grad_agg, 'col', axis=0, tiled=True)  74.3 us
    psum x1, blocking collectives, axis_by_axis(): partial = lax.psum(x, inner_axis)  68.4 us
    psum x1, waiting for transfers between devices, axis_by_axis(): return lax.psum(partial, outer_axis)  47.6 us
    psum x1, blocking collectives, axis_by_axis(): return lax.psum(partial, outer_axis)  35.2 us
  transfers between devices with their start and end apart: 6, of which 5 were waited for; matrix products, arithmetic and copies ran while one was open for 1% of the time, Pallas kernels for 0%

profile of v1, /device:TPU:8, one launch (start us, length us, event | category | flops | bytes accessed | tf_op | source)
XLA Modules:
  0.0 763.7 jit_solution(12115475459545178392)
XLA Ops:
  7.2 0.7 all-gather.3.cloned.1.call-update
  10.0 97.8 %all-gather.3.cloned.1.call-done = bf16[4096,512]{1,0:T(8,128)(2,1)} async-done(((bf16[128,512]{1,0:T(8,128)(2,1)}), bf16[4096,512]{1,0:T(8,128)(2,1)}) %all-gather.3.cloned.1.call-update) | async-done | bytes 4194320 | tf_op jit(solution)/shard_map/all_gather | solution.py:76
  107.8 2.8 gather_fusion
  110.6 2.4 convolution_bitcast_fusion.1
  113.0 5.3 copy.18
  118.3 4.3 convolution_convert_fusion.1
  122.6 2.5 copy.19
  125.2 76.2 %reduce-scatter.2.cloned.1.call-done = bf16[128,512]{1,0:T(8,128)(2,1)} async-done(((bf16[2048,512]{1,0:T(8,128)(2,1)}), bf16[128,512]{1,0:T(8,128)(2,1)}) %reduce-scatter.2.cloned.1.call-update) | async-done | bytes 131088 | tf_op jit(solution)/shard_map/reduce_scatter | solution.py:81
  201.4 1.9 fusion.25
  203.3 1.0 convolution_convert_fusion.2
  204.3 74.3 %all-gather.5.cloned.1.call-done = bf16[2048,512]{1,0:T(8,128)(2,1)} async-done(((bf16[128,512]{1,0:T(8,128)(2,1)}), bf16[2048,512]{1,0:T(8,128)(2,1)}) %all-gather.5.cloned.1.call-update) | async-done | bytes 2097168 | tf_op jit(solution)/shard_map/all_gather | solution.py:94
  278.6 2.2 gather_fusion.1
  280.9 2.4 convolution_bitcast_fusion
  283.3 5.3 copy.21
  288.5 5.5 convolution_convert_fusion
  294.0 4.4 copy.22
  298.4 9.9 %all-to-all-start = ((bf16[32,128,512]{2,1,0:T(8,128)(2,1)}), bf16[32,128,512]{2,1,0:T(8,128)(2,1)}, u32[]{:S(2)}, u32[]{:S(2)}) async-start(bf16[32,128,512]{2,1,0:T(8,128)(2,1)} %copy.22), calls=%async_computation.1 | async-start | bytes 8388608 | tf_op jit(solution)/shard_map/all_to_all | solution.py:97
  308.4 1.3 fusion.9
  309.7 290.5 %all-reduce.3.cloned.1.call-done = f32[512,512]{1,0:T(8,128)} async-done(((f32[512,512]{1,0:T(8,128)}), f32[512,512]{1,0:T(8,128)}) %all-reduce.3.cloned.1.call-update) | async-done | bytes 1048592 | tf_op jit(solution)/shard_map/psum | solution.py:8
  600.3 68.4 %psum.30 = f32[512]{0:T(512)S(1)} all-reduce(f32[512]{0:T(512)S(1)} %get-tuple-element.36), channel_id=1, replica_groups=mesh['row'=32,'col'=16] {'row'}, use_global_device_ids=true, to_apply=%region_4.5 | all-reduce | flops 512 | bytes 4096 | tf_op jit(solution)/shard_map/psum | solution.py:8
  668.7 35.2 %psum.31 = f32[512]{0:T(512)} all-reduce(f32[512]{0:T(512)S(1)} %psum.30), channel_id=1, replica_groups=mesh['row'=32,'col'=16] {'col'}, use_global_device_ids=true, to_apply=%region_5.6 | all-reduce | flops 512 | bytes 4096 | tf_op jit(solution)/shard_map/psum | solution.py:9
  703.9 3.5 reduce_sum.22
  707.4 47.6 %all-reduce.5.cloned.1.call-done = f32[512,512]{1,0:T(8,128)} async-done(((f32[512,512]{1,0:T(8,128)}), f32[512,512]{1,0:T(8,128)}) %all-reduce.5.cloned.1.call-update) | async-done | bytes 1048592 | tf_op jit(solution)/shard_map/psum | solution.py:9
  755.0 2.3 copy.28
  (31 shorter events, 1.7 us)
Async XLA Ops:
  7.2 194.2 %copy-start = (bf16[512,512]{1,0:T(8,128)(2,1)S(1)}, bf16[512,512]{1,0:T(8,128)(2,1)}, u32[]{:S(2)}) copy-start(bf16[512,512]{1,0:T(8,128)(2,1)} %param.13) | copy-start | bytes 1572868
  7.2 103.4 %copy-start.1 = (bf16[1,1,12,128,128]{4,3,2,1,0:T(8,128)(2,1)S(1)}, bf16[1,1,12,128,128]{4,3,2,1,0:T(8,128)(2,1)}, u32[]{:S(2)}) copy-start(bf16[1,1,12,128,128]{4,3,2,1,0:T(8,128)(2,1)} %param.9) | copy-start | bytes 1179652
  7.2 100.6 %all-gather.3.cloned.1.call-start = ((), (), s32[]{:S(2)}) async-start(), calls=%async_computation.2 | async-start | bytes 4325376 | tf_op jit(solution)/shard_map/all_gather | solution.py:76
  7.9 193.4 %reduce-scatter.2.cloned.1.call-start = ((), (), s32[]{:S(2)}) async-start(), calls=%async_computation.3 | async-start | bytes 2228224 | tf_op jit(solution)/shard_map/reduce_scatter | solution.py:81
  113.0 5.3 copy-start.4
  125.1 76.3 %copy-start.5 = (bf16[128,512]{1,0:T(8,128)(2,1)S(1)}, bf16[128,512]{1,0:T(8,128)(2,1)}, u32[]{:S(2)}) copy-start(bf16[128,512]{1,0:T(8,128)(2,1)} %param.15) | copy-start | bytes 393220
  125.1 76.3 %copy-start.6 = (f32[512]{0:T(512)S(1)}, f32[512]{0:T(512)}, u32[]{:S(2)}) copy-start(f32[512]{0:T(512)} %param.14) | copy-start | bytes 6148
  125.1 153.5 %all-gather.5.cloned.1.call-start = ((), (), s32[]{:S(2)}) async-start(), calls=%async_computation.6 | async-start | bytes 2228224 | tf_op jit(solution)/shard_map/all_gather | solution.py:94
  283.3 5.3 copy-start.3
  298.4 10.0 %copy-start.2 = (bf16[128,512]{1,0:T(8,128)(2,1)S(1)}, bf16[128,512]{1,0:T(8,128)(2,1)}, u32[]{:S(2)}) copy-start(bf16[128,512]{1,0:T(8,128)(2,1)} %reduce-scatter.2.cloned.1.call-done) | copy-start | bytes 393220
  298.4 405.5 %all-to-all-start = ((bf16[32,128,512]{2,1,0:T(8,128)(2,1)}), bf16[32,128,512]{2,1,0:T(8,128)(2,1)}, u32[]{:S(2)}, u32[]{:S(2)}) async-start(bf16[32,128,512]{2,1,0:T(8,128)(2,1)} %copy.22), calls=%async_computation.1 | async-start | bytes 8388608 | tf_op jit(solution)/shard_map/all_to_all | solution.py:97
  308.3 291.9 %all-reduce.3.cloned.1.call-start = ((), (), s32[]{:S(2)}) async-start(), calls=%async_computation.4 | async-start | bytes 2097152 | tf_op jit(solution)/shard_map/psum | solution.py:8
  309.7 445.3 %all-reduce.5.cloned.1.call-start = ((), (), s32[]{:S(2)}) async-start(), calls=%async_computation.5 | async-start | bytes 2097152 | tf_op jit(solution)/shard_map/psum | solution.py:9
Sparse Core Ops, SparseCore 0:
  11.4 96.3 all-gather.2
  125.3 76.0 reduce-scatter.1
  204.4 74.1 all-gather.4
  312.3 287.8 all-reduce.2
  603.3 151.6 all-reduce.4
